TPU v7x, 32 devices: a whole 2x2x4 slice. The times are simulated.
32 devices in a mesh: groups: 2 (over y), rows: 4 (over x, core), cols: 4 (over z).
Axes of the slice: x: 2, y: 2, z: 4, core: 2. Of those that a mesh axis runs over, the one named last changes fastest.
Arguments:
- pair_rep: float32 [384, 192, 128], P(('groups', 'cols'), 'rows'), parts along dimension 0, may hold values from -6 to 6
- token_mask: int32 [384], P(('groups', 'rows')), parts along dimension 0, may hold values from 0 to 1, as said below
- norm_gain: float32 [128], replicated, may hold values from 0.1 to 1.9
- norm_shift: float32 [128], replicated, may hold values from -3 to 3
- w_query: bfloat16 [128, 128], replicated, may hold values from -0.5 to 0.5
- w_keyval: bfloat16 [128, 256], replicated, may hold values from -0.5 to 0.5
- w_gate: bfloat16 [128, 128], replicated, may hold values from -0.5 to 0.5
- gate_shift: float32 [128], replicated, may hold values from -3 to 3
- w_bias: float32 [128, 4], replicated, may hold values from -12 to 12
- w_out: bfloat16 [128, 128], replicated, may hold values from -0.5 to 0.5
- out_shift: float32 [128], replicated, may hold values from -3 to 3
Outputs:
- pair_update: float32 [384, 192, 128], P(('groups', 'cols'), 'rows'), parts along dimension 0
There are 2 independent parts, one for each index of `groups`. A program takes and returns all parts, laid end to end along the dimension named above; an argument that names none is the same for every part. Nothing has to cross between parts.
Inputs may be any that keep to these rules, and one draw needn't show every extreme that they name: `token_mask`: position 0 is always a valid residue and the last position never is.
All inputs are finite; a program needn't handle non-finite values.
Results may differ from a plain program's by a relative error of at most 0.012.
The roundings to bfloat16 on the way count: a program that leaves them out, or rounds other values in their place, can miss the bound.
Values may be sent and summed in bfloat16 or wider, within the bound.
No kernel may reach another device: no remote copies, remote signals or barrier semaphores. Data moves between devices by JAX's collectives and lax.ppermute only.
A program may use at most 128 MiB of HBM per device.

v0:
```python
import jax
import jax.numpy as jnp
from jax import lax
from jax.sharding import PartitionSpec as P

HEADS = 4
HEAD_DIM = 32


def layer_norm(values, norm_gain, norm_shift):
    mean_val = jnp.mean(values, axis=-1, keepdims=True)
    centred = values - mean_val
    variance = jnp.mean(centred * centred, axis=-1, keepdims=True)
    return (centred * lax.rsqrt(variance + 1e-05) * norm_gain + norm_shift).astype(jnp.bfloat16)


def largest_divisor(count, limit):
    return max(
        (candidate for candidate in range(1, min(count, limit) + 1) if count % candidate == 0)
    )


def whole_row_layer(
    normed, token_mask, w_query, w_keyval, w_gate, gate_shift, w_bias, w_out, out_shift
):
    width = normed.shape[2]
    local_bias = jnp.dot(
        normed.astype(jnp.float32), w_bias, precision=lax.Precision.HIGHEST
    ).transpose(2, 0, 1)
    wide = lax.all_to_all(normed, "rows", split_axis=0, concat_axis=1, tiled=True)
    few_rows, token_count, _ = wide.shape
    bias_part = lax.all_gather(local_bias, "cols", axis=1, tiled=True)
    full_bias, full_mask = (
        lax.all_gather(bias_part, "rows", axis=2, tiled=True),
        lax.all_gather(token_mask.astype(jnp.float32), "rows", axis=0, tiled=True),
    )
    queries = (
        jnp.dot(wide, w_query, preferred_element_type=jnp.float32) * HEAD_DIM ** (-0.5)
    ).astype(jnp.bfloat16)
    queries = queries.reshape(few_rows, token_count, HEADS, HEAD_DIM)
    keyvals = jnp.dot(wide, w_keyval, preferred_element_type=jnp.float32).astype(jnp.bfloat16)
    keys = keyvals[..., :width].reshape(few_rows, token_count, HEADS, HEAD_DIM)
    values = keyvals[..., width:].reshape(few_rows, token_count, HEADS, HEAD_DIM)
    gates = jax.nn.sigmoid(jnp.dot(wide, w_gate, preferred_element_type=jnp.float32) + gate_shift)
    usable = full_mask > 0.5
    block_len = largest_divisor(token_count, 128)

    def one_block(block_index, gated_all):
        start = block_index * block_len
        query_block = lax.dynamic_slice_in_dim(queries, start, block_len, 1)
        bias_block = lax.dynamic_slice_in_dim(full_bias, start, block_len, 1)
        gate_block = lax.dynamic_slice_in_dim(gates, start, block_len, 1)
        scores = jnp.einsum(
            "ijhd,ikhd->hijk", query_block, keys, preferred_element_type=jnp.float32
        )
        scores = scores + bias_block[:, None]
        scores = jnp.where(usable[None, None, None, :], scores, jnp.float32(-1000000000.0))
        highest = jnp.max(scores, axis=-1, keepdims=True)
        expo = jnp.exp(scores - highest)
        total = jnp.sum(expo, axis=-1)
        weights = expo.astype(jnp.bfloat16)
        mixed = jnp.einsum("hijk,ikhd->ijhd", weights, values, preferred_element_type=jnp.float32)
        attended = mixed / total.transpose(1, 2, 0)[..., None]
        gated = (gate_block * attended.reshape(few_rows, block_len, width)).astype(jnp.bfloat16)
        return lax.dynamic_update_slice_in_dim(gated_all, gated, start, 1)

    gated_all = lax.fori_loop(
        0,
        token_count // block_len,
        one_block,
        jnp.zeros((few_rows, token_count, width), jnp.bfloat16),
    )
    gated_home = lax.all_to_all(gated_all, "rows", split_axis=1, concat_axis=0, tiled=True)
    return jnp.dot(gated_home, w_out, preferred_element_type=jnp.float32) + out_shift


def on_device(
    pair_rep,
    token_mask,
    norm_gain,
    norm_shift,
    w_query,
    w_keyval,
    w_gate,
    gate_shift,
    w_bias,
    w_out,
    out_shift,
):
    normed = layer_norm(pair_rep, norm_gain, norm_shift)
    return whole_row_layer(
        normed, token_mask, w_query, w_keyval, w_gate, gate_shift, w_bias, w_out, out_shift
    )


def solution(mesh):
    return jax.shard_map(
        on_device,
        mesh=mesh,
        in_specs=(
            P(("groups", "cols"), "rows", None),
            P(("groups", "rows")),
            P(),
            P(),
            P(),
            P(),
            P(),
            P(),
            P(),
            P(),
            P(),
        ),
        out_specs=P(("groups", "cols"), "rows", None),
        check_vma=False,
    )
```

profile of v0, /device:TPU:0, one launch (start us, length us, event | category | flops | bytes accessed | tf_op | source)
XLA Modules:
  0.0 85.9 jit_solution(3610924705760710887)
XLA Ops:
  0.0 1.7 %reduce_sum.31 = f32[48,48]{1,0:T(8,128)S(1)} reduce(f32[48,48,128]{2,1,0:T(8,128)} %param.13, f32[]{:T(128)} %constant.58.clone.1), dimensions={2}, to_apply=%region_0.0 | reduce | flops 292608 | bytes 1188868 | tf_op jit(solution)/shard_map/reduce_sum | solution.py:11
  1.8 0.7 multiply_reduce_fusion
  2.5 1.5 %add_convert_fusion = bf16[48,48,128]{2,1,0:T(8,128)(2,1)} fusion(f32[48,48,128]{2,1,0:T(8,128)S(1)} %copy-done.1, f32[128]{0:T(128)S(1)} %copy-done.8, f32[128]{0:T(128)S(1)} %copy-done.9, f32[48,48]{1,0:T(8,128)S(1)} %add_rsqrt_fusion, f32[48,48]{1,0:T(8,128)S(1)} %broadcast_multiply_fusion), kind=kLoop, calls=%fused_computation.31 | loop fusion | flops 1474560 | bytes 1788928 | tf_op jit(solution)/shard_map/convert_element_type | solution.py:14
  4.0 4.2 %all-to-all-start = ((bf16[48,48,128]{2,1,0:T(8,128)(2,1)}), bf16[48,48,128]{2,1,0:T(8,128)(2,1)S(1)}, u32[]{:S(2)}, u32[]{:S(2)}) async-start(bf16[48,48,128]{2,1,0:T(8,128)(2,1)} %add_convert_fusion), calls=%async_computation | async-start | bytes 1179648 | tf_op jit(solution)/shard_map/all_to_all | solution.py:30
  8.3 2.8 %convolution_bitcast_fusion = f32[4,48,48]{2,0,1:T(4,128)S(1)} fusion(bf16[48,48,128]{2,1,0:T(8,128)(2,1)} %add_convert_fusion, f32[128,4]{0,1:T(4,128)S(1)} %copy-done.7), kind=kOutput, calls=%fused_computation.33 | convolution fusion | flops 14155776 | bytes 628736 | tf_op jit(solution)/shard_map/dot_general | solution.py:27
  11.1 15.8 %all_gather.10 = f32[4,192,48]{2,0,1:T(4,128)S(1)} all-gather(f32[4,48,48]{2,0,1:T(4,128)S(1)} %convolution_bitcast_fusion), channel_id=1, replica_groups=mesh['groups'=2,'rows'=4,'cols'=4] {'cols'}, dimensions={1}, use_global_device_ids=true | all-gather | bytes 184320 | tf_op jit(solution)/shard_map/all_gather | solution.py:32
  27.2 0.6 dynamic-slice
  28.4 5.6 %all-reduce = f32[192]{0:T(256)S(1)} all-reduce(f32[192]{0:T(256)S(1)} %convert_dynamic-update-slice_fusion), channel_id=1, replica_groups=mesh['groups'=2,'rows'=4,'cols'=4] {'rows'}, use_global_device_ids=true, to_apply=%add | all-reduce | flops 192 | bytes 1536
  34.1 9.0 %all_gather.11 = f32[4,192,192]{1,0,2:T(4,128)S(1)} all-gather(f32[4,192,48]{1,0,2:T(4,128)S(1)} %copy.36), channel_id=1, replica_groups=mesh['groups'=2,'rows'=4,'cols'=4] {'rows'}, dimensions={2}, use_global_device_ids=true | all-gather | bytes 737280 | tf_op jit(solution)/shard_map/all_gather | solution.py:34
  43.2 0.4 convolution_convert_fusion
  43.7 0.3 fusion.39
  44.0 0.3 copy.35
  44.3 0.9 %copy.40 = bf16[12,192,4,32]{1,3,0,2:T(8,128)(2,1)} copy(bf16[12,192,4,32]{1,3,2,0:T(8,128)(2,1)S(1)} %bitcast.59) | data formatting | bytes 1179648 | tf_op jit(solution)/shard_map/while | solution.py:67
  45.2 1.2 %copy.37 = bf16[12,192,128]{1,2,0:T(8,128)(2,1)} copy(bf16[12,192,128]{2,1,0:T(8,128)(2,1)S(1)} %get-tuple-element.188) | data formatting | bytes 1179648 | tf_op jit(solution)/shard_map/slice | solution.py:43
  46.4 0.3 fusion.28
  46.7 1.2 %copy.34 = bf16[12,192,128]{1,2,0:T(8,128)(2,1)} copy(bf16[12,192,128]{2,1,0:T(8,128)(2,1)S(1)} %fusion.28) | data formatting | bytes 1179648 | tf_op jit(solution)/shard_map/convert_element_type | solution.py:39
  47.9 1.5 %fusion.27 = f32[12,192,128]{2,1,0:T(8,128)} fusion(bf16[12,192,128]{2,1,0:T(8,128)(2,1)S(1)} %bitcast.58, f32[128]{0:T(128)S(1)} %copy-done.13, bf16[128,128]{1,0:T(8,128)(2,1)S(1)} %copy-done.11), kind=kOutput, calls=%fused_computation.29 | convolution fusion | flops 76677120 | bytes 1802752 | tf_op jit(solution)/shard_map/dot_general | solution.py:44
  49.3 1.0 %broadcast_in_dim.45.clone = bf16[12,192,128]{2,0,1:T(8,128)(2,1)} broadcast(bf16[]{:T(256)} %constant.57.clone.1), dimensions={} | broadcast | bytes 589826 | tf_op jit(solution)/shard_map/broadcast_in_dim | solution.py:71
  50.3 18.9 %while.13 = (s32[]{:T(128)}, bf16[12,192,128]{2,0,1:T(8,128)(2,1)}, f32[12,192,128]{2,1,0:T(8,128)}, pred[192]{0:T(512)(128)(4,1)S(1)}, bf16[12,192,4,32]{1,3,2,...) while((s32[]{:T(128)}, bf16[12,192,128]{2,0,1:T(8,128)(2,1)}, ...), condition=%wide.region_5.6_spmd, body=%wide.region_2.5_spmd.sunk | while | flops 118112448 | bytes 19440052 | solution.py:67
  50.3 0.3 constant_dynamic-slice_fusion.13
  50.8 4.4 %fusion.59 = (f32[4,12,96]{2,1,0:T(8,128)S(1)}, bf16[4,12,96,192]{3,2,1,0:T(8,128)(2,1)}) fusion(f32[4,96,192]{2,1,0:T(8,128)S(1)} %copy.78, pred[192]{0:T(512)(128)(4,1)S(1)} %get-tuple-element.270, bf16[12,192,4,32]{1,3,0,2:T(8,128)(2,1)S(1)} %get-tuple-element.272, bf16[12,192,4,32]{1,3,2,0:T(8,128)(2,1)} %get-tuple-element.271, s32[]{:T(128)S(6)} %select_n.31), kind=kOutput, calls=%fused_computation.43.clone.1 | convolution fusion | flops 61046976 | bytes 3066052 | tf_op jit(solution)/shard_map/while/body/eval_jaxpr/sub | solution.py:59
  55.3 2.9 %fusion.60 = f32[12,96,4,32]{1,3,2,0:T(8,128)S(1)} fusion(bf16[12,192,4,32]{1,3,2,0:T(8,128)(2,1)} %get-tuple-element.274, bf16[4,12,96,192]{3,2,1,0:T(8,128)(2,1)} %get-tuple-element.241, f32[12,96,4]{1,2,0:T(4,128)S(1)} %copy.79), kind=kOutput, calls=%fused_computation.10.clone.1 | convolution fusion | flops 56770560 | bytes 2967552 | tf_op jit(solution)/shard_map/while/body/eval_jaxpr/hijk,ikhd->ijhd/dot_general | solution.py:62
  58.3 0.3 copy.77
  58.6 0.3 copy.80
  59.0 0.8 constant_dynamic-update-slice_fusion.2
  59.8 0.3 constant_dynamic-slice_fusion.13
  60.3 4.4 %fusion.59 = (f32[4,12,96]{2,1,0:T(8,128)S(1)}, bf16[4,12,96,192]{3,2,1,0:T(8,128)(2,1)}) fusion(f32[4,96,192]{2,1,0:T(8,128)S(1)} %copy.78, pred[192]{0:T(512)(128)(4,1)S(1)} %get-tuple-element.270, bf16[12,192,4,32]{1,3,0,2:T(8,128)(2,1)S(1)} %get-tuple-element.272, bf16[12,192,4,32]{1,3,2,0:T(8,128)(2,1)} %get-tuple-element.271, s32[]{:T(128)S(6)} %select_n.31), kind=kOutput, calls=%fused_computation.43.clone.1 | convolution fusion | flops 61046976 | bytes 3066052 | tf_op jit(solution)/shard_map/while/body/eval_jaxpr/sub | solution.py:59
  64.7 2.9 %fusion.60 = f32[12,96,4,32]{1,3,2,0:T(8,128)S(1)} fusion(bf16[12,192,4,32]{1,3,2,0:T(8,128)(2,1)} %get-tuple-element.274, bf16[4,12,96,192]{3,2,1,0:T(8,128)(2,1)} %get-tuple-element.241, f32[12,96,4]{1,2,0:T(4,128)S(1)} %copy.79), kind=kOutput, calls=%fused_computation.10.clone.1 | convolution fusion | flops 56770560 | bytes 2967552 | tf_op jit(solution)/shard_map/while/body/eval_jaxpr/hijk,ikhd->ijhd/dot_general | solution.py:62
  68.1 0.3 copy.80
  68.4 0.8 constant_dynamic-update-slice_fusion.2
  69.2 15.2 %all_to_all.36 = bf16[12,192,128]{2,0,1:T(8,128)(2,1)S(1)} all-to-all(bf16[12,192,128]{2,0,1:T(8,128)(2,1)} %get-tuple-element.281), channel_id=1, replica_groups=mesh['groups'=2,'rows'=4,'cols'=4] {'rows'}, dimensions={1} | all-to-all | bytes 1179648 | tf_op jit(solution)/shard_map/all_to_all | solution.py:73
  84.6 1.3 %convolution_add_fusion = f32[48,48,128]{2,1,0:T(8,128)} fusion(bf16[48,48,128]{2,1,0:T(8,128)(2,1)S(1)} %bitcast.62, f32[128]{0:T(128)S(1)} %copy-done.10, bf16[128,128]{1,0:T(8,128)(2,1)S(1)} %copy-done.5), kind=kOutput, calls=%fused_computation.23 | convolution fusion | flops 75792384 | bytes 1802752 | tf_op jit(solution)/shard_map/dot_general | solution.py:74
  (52 shorter events, 1.6 us)
Async XLA Ops:
  0.0 43.2 %copy-start = (bf16[128,256]{1,0:T(8,128)(2,1)S(1)}, bf16[128,256]{1,0:T(8,128)(2,1)}, u32[]{:S(2)}) copy-start(bf16[128,256]{1,0:T(8,128)(2,1)} %param.18) | copy-start | bytes 196612
  0.0 1.8 %copy-start.1 = (f32[48,48,128]{2,1,0:T(8,128)S(1)}, f32[48,48,128]{2,1,0:T(8,128)}, u32[]{:S(2)}) copy-start(f32[48,48,128]{2,1,0:T(8,128)} %param.13) | copy-start | bytes 3538948
  0.0 2.5 %copy-start.9 = (f32[128]{0:T(128)S(1)}, f32[128]{0:T(128)}, u32[]{:S(2)}) copy-start(f32[128]{0:T(128)} %param.15) | copy-start | bytes 1540
  0.0 2.5 %copy-start.8 = (f32[128]{0:T(128)S(1)}, f32[128]{0:T(128)}, u32[]{:S(2)}) copy-start(f32[128]{0:T(128)} %param.16) | copy-start | bytes 1540
  2.5 5.8 %copy-start.7 = (f32[128,4]{0,1:T(4,128)S(1)}, f32[128,4]{0,1:T(4,128)}, u32[]{:S(2)}) copy-start(f32[128,4]{0,1:T(4,128)} %param.21) | copy-start | bytes 6148
  4.0 39.1 %all-to-all-start = ((bf16[48,48,128]{2,1,0:T(8,128)(2,1)}), bf16[48,48,128]{2,1,0:T(8,128)(2,1)S(1)}, u32[]{:S(2)}, u32[]{:S(2)}) async-start(bf16[48,48,128]{2,1,0:T(8,128)(2,1)} %add_convert_fusion), calls=%async_computation | async-start | bytes 1179648 | tf_op jit(solution)/shard_map/all_to_all | solution.py:30
  8.3 18.9 %copy-start.14 = (u32[32]{0:T(128)S(1)}, u32[32]{0:T(128)}, u32[]{:S(2)}) copy-start(u32[32]{0:T(128)} %constant.66) | copy-start | bytes 388
  8.3 20.1 %copy-start.12 = (s32[48]{0:T(128)S(1)}, s32[48]{0:T(128)}, u32[]{:S(2)}) copy-start(s32[48]{0:T(128)} %param.14) | copy-start | bytes 580
  44.3 2.1 %copy-start.6 = (bf16[128,128]{1,0:T(8,128)(2,1)S(1)}, bf16[128,128]{1,0:T(8,128)(2,1)}, u32[]{:S(2)}) copy-start(bf16[128,128]{1,0:T(8,128)(2,1)} %param.17) | copy-start | bytes 98308
  46.4 1.5 %copy-start.11 = (bf16[128,128]{1,0:T(8,128)(2,1)S(1)}, bf16[128,128]{1,0:T(8,128)(2,1)}, u32[]{:S(2)}) copy-start(bf16[128,128]{1,0:T(8,128)(2,1)} %param.19) | copy-start | bytes 98308
  46.4 1.5 %copy-start.13 = (f32[128]{0:T(128)S(1)}, f32[128]{0:T(128)}, u32[]{:S(2)}) copy-start(f32[128]{0:T(128)} %param.20) | copy-start | bytes 1540
  47.9 2.5 %copy-start.3 = (bf16[12,192,4,32]{1,3,0,2:T(8,128)(2,1)S(1)}, bf16[12,192,4,32]{1,3,0,2:T(8,128)(2,1)}, u32[]{:S(2)}) copy-start(bf16[12,192,4,32]{1,3,0,2:T(8,128)(2,1)} %copy.40) | copy-start | bytes 1769476
  55.3 2.9 %copy-start.2 = (f32[12,192,128]{2,1,0:T(8,128)S(1)}, f32[12,192,128]{2,1,0:T(8,128)}, u32[]{:S(2)}) copy-start(f32[12,192,128]{2,1,0:T(8,128)} %get-tuple-element.269) | copy-start | bytes 3538948 | tf_op jit(solution)/shard_map/while
  58.6 1.2 %copy-start.4 = (bf16[12,192,4,32]{1,3,0,2:T(8,128)(2,1)S(1)}, bf16[12,192,4,32]{1,3,0,2:T(8,128)(2,1)}, u32[]{:S(2)}) copy-start(bf16[12,192,4,32]{1,3,0,2:T(8,128)(2,1)} %get-tuple-element.292) | copy-start | bytes 1769476 | tf_op jit(solution)/shard_map/while
  64.7 2.9 %copy-start.2 = (f32[12,192,128]{2,1,0:T(8,128)S(1)}, f32[12,192,128]{2,1,0:T(8,128)}, u32[]{:S(2)}) copy-start(f32[12,192,128]{2,1,0:T(8,128)} %get-tuple-element.269) | copy-start | bytes 3538948 | tf_op jit(solution)/shard_map/while
  68.1 1.1 %copy-start.4 = (bf16[12,192,4,32]{1,3,0,2:T(8,128)(2,1)S(1)}, bf16[12,192,4,32]{1,3,0,2:T(8,128)(2,1)}, u32[]{:S(2)}) copy-start(bf16[12,192,4,32]{1,3,0,2:T(8,128)(2,1)} %get-tuple-element.292) | copy-start | bytes 1769476 | tf_op jit(solution)/shard_map/while
  69.2 15.4 %copy-start.5 = (bf16[128,128]{1,0:T(8,128)(2,1)S(1)}, bf16[128,128]{1,0:T(8,128)(2,1)}, u32[]{:S(2)}) copy-start(bf16[128,128]{1,0:T(8,128)(2,1)} %param.22) | copy-start | bytes 98308
  69.2 15.4 %copy-start.10 = (f32[128]{0:T(128)S(1)}, f32[128]{0:T(128)}, u32[]{:S(2)}) copy-start(f32[128]{0:T(128)} %param.23) | copy-start | bytes 1540
where the time goes:
time: 86.4 us; the launch traced here: 85.9 us
  blocking collectives  45.7 us (53%)
  matrix products  21 us (24%)
  local copies, waits for them, and re-layouts  9.81 us (11%)
  other arithmetic  4.24 us (5%)
  starting transfers between devices  4.24 us (5%)
    all_gather x1, blocking collectives, whole_row_layer(): bias_part = lax.all_gather(local_bias, 'cols', axis=1, tiled=True)  15.8 us
    all_to_all x1, blocking collectives, whole_row_layer(): lax.all_to_all(gated_all, 'rows', split_axis=1, concat_axis=0, tiled=True)  15.2 us
    all_gather x1, blocking collectives, whole_row_layer(): lax.all_gather(bias_part, 'rows', axis=2, tiled=True)  9.04 us
    sub x2, matrix products, one_block(): expo = jnp.exp(scores - highest)  8.86 us
    dot_general x2, matrix products, one_block(): jnp.einsum('hijk,ikhd->ijhd', weights, values, preferred_element_type=jnp...  5.81 us
    unnamed x1, blocking collectives  5.63 us
    all_to_all x1, starting transfers between devices, whole_row_layer(): lax.all_to_all(normed, 'rows', split_axis=0, concat_axis=1, tiled=True)  4.24 us
    dot_general x1, matrix products, whole_row_layer(): jnp.dot(normed.astype(jnp.float32), w_bias, precision=lax.Precision.HIGHEST)  2.85 us
  transfers between devices with their start and end apart: 1, of which 0 were waited for; matrix products, arithmetic and copies ran while one was open for 4% of the time, Pallas kernels for 0%

commit v1 on v0

--- a/solution.py
+++ b/solution.py
@@ -5,6 +5,13 @@
 
 HEADS = 4
 HEAD_DIM = 32
+
+
+def start_point_by_axis(target, d0):
+    target = jnp.moveaxis(target, 0, d0)
+    b_next = target.shape
+    p_next = target.reshape(*b_next[:d0], b_next[d0] * b_next[d0 + 1], *b_next[d0 + 2 :])
+    return p_next
 
 
 def layer_norm(values, norm_gain, norm_shift):
@@ -29,7 +36,33 @@
     ).transpose(2, 0, 1)
     wide = lax.all_to_all(normed, "rows", split_axis=0, concat_axis=1, tiled=True)
     few_rows, token_count, _ = wide.shape
-    bias_part = lax.all_gather(local_bias, "cols", axis=1, tiled=True)
+    n_dev_all = jax.lax.axis_size("cols")
+    blocks_here = []
+    d = 0
+    while d < n_dev_all:
+        blocks_here.append((d, (d + 1) % n_dev_all))
+        d += 1
+    chunks = []
+    for to_i, i in blocks_here:
+        chunks.append((i, to_i))
+    carry, z_new = ([], [])
+    dd = 0
+    while dd < n_dev_all - 1:
+        if dd % 2 == 0:
+            carry.append(
+                jax.lax.ppermute(
+                    carry[-1] if carry else local_bias, perm=blocks_here, axis_name="cols"
+                )
+            )
+        else:
+            z_new.append(
+                jax.lax.ppermute(z_new[-1] if z_new else local_bias, axis_name="cols", perm=chunks)
+            )
+        dd = dd + 1
+    tile_out = jnp.stack([*carry[::-1], local_bias, *z_new], axis=0)
+    far_arr = jax.lax.axis_index("cols") - len(carry)
+    tile_out = tile_out[(jnp.arange(n_dev_all) - far_arr) % n_dev_all]
+    bias_part = start_point_by_axis(tile_out, 1)
     full_bias, full_mask = (
         lax.all_gather(bias_part, "rows", axis=2, tiled=True),
         lax.all_gather(token_mask.astype(jnp.float32), "rows", axis=0, tiled=True),

time: 86.4 us -> 86.2 us (level)
  blocking collectives: 45.7 us -> 33.4 us
  waiting for transfers between devices: 0.01 us -> 6.38 us
  starting transfers between devices: 4.24 us -> 8.66 us
  local copies, waits for them, and re-layouts: 9.81 us -> 10.8 us
    all_gather x1 -> x0, blocking collectives: 15.8 us -> none  [whole_row_layer(): bias_part = lax.all_gather(local_bias, 'cols', axis=1, tiled=True)]
    ppermute x0 -> x3, waiting for transfers between devices: none -> 6.38 us  [the longest x2 6.38 us: whole_row_layer(): jax.lax.ppermute(carry[-1] if carry else local_bias, perm=blocks_here, ax...]
    ppermute x0 -> x3, starting transfers between devices: none -> 5.18 us  [the longest x2 3.14 us: whole_row_layer(): jax.lax.ppermute(carry[-1] if carry else local_bias, perm=blocks_here, ax...]
    unnamed x1, blocking collectives: 5.63 us -> 9.47 us
  transfers between devices with their start and end apart: 1 -> 4, of which waited for: 0 -> 1; matrix products, arithmetic and copies ran while one was open for 4% -> 2% of each run, Pallas kernels for 0% -> 0%
where the time goes in v1:
time: 86.2 us; the launch traced here: 85.7 us
  blocking collectives  33.4 us (39%)
  matrix products  21.1 us (24%)
  local copies, waits for them, and re-layouts  10.8 us (13%)
  starting transfers between devices  8.66 us (10%)
  waiting for transfers between devices  6.38 us (7%)
  other arithmetic  4.36 us (5%)
  between operations  0.93 us (1%)
    all_to_all x1, blocking collectives, whole_row_layer(): lax.all_to_all(gated_all, 'rows', split_axis=1, concat_axis=0, tiled=True)  15.2 us
    unnamed x1, blocking collectives  9.47 us
    sub x2, matrix products, one_block(): expo = jnp.exp(scores - highest)  8.87 us
    all_gather x1, blocking collectives, whole_row_layer(): lax.all_gather(bias_part, 'rows', axis=2, tiled=True)  8.74 us
    ppermute x2, waiting for transfers between devices, whole_row_layer(): jax.lax.ppermute(carry[-1] if carry else local_bias, perm=blocks_here, ax...  6.38 us
    dot_general x2, matrix products, one_block(): jnp.einsum('hijk,ikhd->ijhd', weights, values, preferred_element_type=jnp...  5.81 us
    all_to_all x1, starting transfers between devices, whole_row_layer(): lax.all_to_all(normed, 'rows', split_axis=0, concat_axis=1, tiled=True)  3.48 us
    ppermute x2, starting transfers between devices, whole_row_layer(): jax.lax.ppermute(carry[-1] if carry else local_bias, perm=blocks_here, ax...  3.14 us
  transfers between devices with their start and end apart: 4, of which 1 were waited for; matrix products, arithmetic and copies ran while one was open for 2% of the time, Pallas kernels for 0%

profile of v1, /device:TPU:0, one launch (start us, length us, event | category | flops | bytes accessed | tf_op | source)
XLA Modules:
  0.0 85.7 jit_solution(9065879832374633326)
XLA Ops:
  0.0 1.7 %reduce_sum.31 = f32[48,48]{1,0:T(8,128)S(1)} reduce(f32[48,48,128]{2,1,0:T(8,128)} %param.13, f32[]{:T(128)} %constant.77.clone.1), dimensions={2}, to_apply=%region_0.0 | reduce | flops 292608 | bytes 1188868 | tf_op jit(solution)/shard_map/reduce_sum | solution.py:18
  1.8 0.7 multiply_reduce_fusion
  2.5 1.5 %add_convert_fusion = bf16[48,48,128]{2,1,0:T(8,128)(2,1)} fusion(f32[48,48,128]{2,1,0:T(8,128)S(1)} %copy-done.1, f32[128]{0:T(128)S(1)} %copy-done.8, f32[128]{0:T(128)S(1)} %copy-done.9, f32[48,48]{1,0:T(8,128)S(1)} %add_rsqrt_fusion, f32[48,48]{1,0:T(8,128)S(1)} %broadcast_multiply_fusion), kind=kLoop, calls=%fused_computation.32 | loop fusion | flops 1474560 | bytes 1788928 | tf_op jit(solution)/shard_map/convert_element_type | solution.py:21
  4.0 2.9 %fusion.33 = f32[48,48,4]{1,2,0:T(4,128)S(1)} fusion(bf16[48,48,128]{2,1,0:T(8,128)(2,1)} %add_convert_fusion, f32[128,4]{0,1:T(4,128)S(1)} %copy-done.7), kind=kOutput, calls=%fused_computation.45 | convolution fusion | flops 14155776 | bytes 628736 | tf_op jit(solution)/shard_map/dot_general | solution.py:34
  6.9 3.1 %collective-permute-start = (f32[4,48,48]{2,0,1:T(4,128)S(1)}, f32[4,48,48]{2,0,1:T(4,128)S(1)}, u32[]{:S(2)}, u32[]{:S(2)}) collective-permute-start(f32[4,48,48]{2,0,1:T(4,128)S(1)} %bitcast.74), channel_id=1, source_target_pairs={{0,1},{1,2},{2,3},{3,0},{4,5},{5,6},{6,7},{7,4},{8,9},{9,10},{10,1... | collective-permute-start | bytes 110600 | tf_op jit(solution)/shard_map/ppermute | solution.py:53
  10.0 2.0 %collective-permute-start.2 = (f32[4,48,48]{2,0,1:T(4,128)S(1)}, f32[4,48,48]{2,0,1:T(4,128)S(1)}, u32[]{:S(2)}, u32[]{:S(2)}) collective-permute-start(f32[4,48,48]{2,0,1:T(4,128)S(1)} %bitcast.75), channel_id=1, source_target_pairs={{1,0},{2,1},{3,2},{0,3},{5,4},{6,5},{7,6},{4,7},{9,8},{10,9},{11,1... | collective-permute-start | bytes 110600 | tf_op jit(solution)/shard_map/ppermute | solution.py:59
  12.0 3.5 %all-to-all-start = ((bf16[48,48,128]{2,1,0:T(8,128)(2,1)}), bf16[48,48,128]{2,1,0:T(8,128)(2,1)S(1)}, u32[]{:S(2)}, u32[]{:S(2)}) async-start(bf16[48,48,128]{2,1,0:T(8,128)(2,1)} %add_convert_fusion), calls=%async_computation | async-start | bytes 1179648 | tf_op jit(solution)/shard_map/all_to_all | solution.py:37
  15.5 0.7 dynamic-slice
  17.0 9.5 %all-reduce = f32[192]{0:T(256)S(1)} all-reduce(f32[192]{0:T(256)S(1)} %convert_dynamic-update-slice_fusion), channel_id=1, replica_groups=mesh['groups'=2,'rows'=4,'cols'=4] {'rows'}, use_global_device_ids=true, to_apply=%add | all-reduce | flops 192 | bytes 1536
  26.6 6.4 %collective-permute-done.1 = f32[4,48,48]{2,0,1:T(4,128)S(1)} collective-permute-done((f32[4,48,48]{2,0,1:T(4,128)S(1)}, f32[4,48,48]{2,0,1:T(4,128)S(1)}, u32[]{:S(2)}, u32[]{:S(2)}) %collective-permute-start.1) | collective-permute-done | bytes 36896 | tf_op jit(solution)/shard_map/ppermute | solution.py:53
  33.1 0.8 gather_fusion
  34.1 8.7 %all_gather.7 = f32[4,192,192]{1,0,2:T(4,128)S(1)} all-gather(f32[4,192,48]{1,0,2:T(4,128)S(1)} %copy.36), channel_id=1, replica_groups=mesh['groups'=2,'rows'=4,'cols'=4] {'rows'}, dimensions={2}, use_global_device_ids=true | all-gather | bytes 737280 | tf_op jit(solution)/shard_map/all_gather | solution.py:67
  42.9 0.4 convolution_convert_fusion
  43.3 0.3 fusion.42
  43.7 0.3 copy.35
  44.0 1.0 %copy.40 = bf16[12,192,4,32]{1,3,0,2:T(8,128)(2,1)} copy(bf16[12,192,4,32]{1,3,2,0:T(8,128)(2,1)S(1)} %bitcast.68) | data formatting | bytes 1179648 | tf_op jit(solution)/shard_map/while | solution.py:100
  44.9 1.2 %copy.37 = bf16[12,192,128]{1,2,0:T(8,128)(2,1)} copy(bf16[12,192,128]{2,1,0:T(8,128)(2,1)S(1)} %get-tuple-element.188) | data formatting | bytes 1179648 | tf_op jit(solution)/shard_map/slice | solution.py:76
  46.1 0.3 fusion.28
  46.4 1.2 %copy.34 = bf16[12,192,128]{1,2,0:T(8,128)(2,1)} copy(bf16[12,192,128]{2,1,0:T(8,128)(2,1)S(1)} %fusion.28) | data formatting | bytes 1179648 | tf_op jit(solution)/shard_map/convert_element_type | solution.py:72
  47.6 1.5 %fusion.27 = f32[12,192,128]{2,1,0:T(8,128)} fusion(bf16[12,192,128]{2,1,0:T(8,128)(2,1)S(1)} %bitcast.67, f32[128]{0:T(128)S(1)} %copy-done.13, bf16[128,128]{1,0:T(8,128)(2,1)S(1)} %copy-done.11), kind=kOutput, calls=%fused_computation.30 | convolution fusion | flops 76677120 | bytes 1802752 | tf_op jit(solution)/shard_map/dot_general | solution.py:77
  49.1 1.0 %broadcast_in_dim.46.clone = bf16[12,192,128]{2,0,1:T(8,128)(2,1)} broadcast(bf16[]{:T(256)} %constant.76.clone.1), dimensions={} | broadcast | bytes 589826 | tf_op jit(solution)/shard_map/broadcast_in_dim | solution.py:104
  50.1 18.9 %while.13 = (s32[]{:T(128)}, bf16[12,192,128]{2,0,1:T(8,128)(2,1)}, f32[12,192,128]{2,1,0:T(8,128)}, pred[192]{0:T(512)(128)(4,1)S(1)}, bf16[12,192,4,32]{1,3,2,...) while((s32[]{:T(128)}, bf16[12,192,128]{2,0,1:T(8,128)(2,1)}, ...), condition=%wide.region_5.6_spmd, body=%wide.region_2.5_spmd.sunk | while | flops 118112448 | bytes 19440052 | solution.py:100
  50.6 4.4 %fusion.62 = (f32[4,12,96]{2,1,0:T(8,128)S(1)}, bf16[4,12,96,192]{3,2,1,0:T(8,128)(2,1)}) fusion(f32[4,96,192]{2,1,0:T(8,128)S(1)} %copy.78, pred[192]{0:T(512)(128)(4,1)S(1)} %get-tuple-element.270, bf16[12,192,4,32]{1,3,0,2:T(8,128)(2,1)S(1)} %get-tuple-element.272, bf16[12,192,4,32]{1,3,2,0:T(8,128)(2,1)} %get-tuple-element.271, s32[]{:T(128)S(6)} %select_n.65), kind=kOutput, calls=%fused_computation.52.clone.1 | convolution fusion | flops 61046976 | bytes 3066052 | tf_op jit(solution)/shard_map/while/body/eval_jaxpr/sub | solution.py:92
  55.0 2.9 %fusion.63 = f32[12,96,4,32]{1,3,2,0:T(8,128)S(1)} fusion(bf16[12,192,4,32]{1,3,2,0:T(8,128)(2,1)} %get-tuple-element.274, bf16[4,12,96,192]{3,2,1,0:T(8,128)(2,1)} %get-tuple-element.241, f32[12,96,4]{1,2,0:T(4,128)S(1)} %copy.79), kind=kOutput, calls=%fused_computation.11.clone.1 | convolution fusion | flops 56770560 | bytes 2967552 | tf_op jit(solution)/shard_map/while/body/eval_jaxpr/hijk,ikhd->ijhd/dot_general | solution.py:95
  58.4 0.3 copy.80
  58.7 0.8 constant_dynamic-update-slice_fusion.2
  60.0 4.4 %fusion.62 = (f32[4,12,96]{2,1,0:T(8,128)S(1)}, bf16[4,12,96,192]{3,2,1,0:T(8,128)(2,1)}) fusion(f32[4,96,192]{2,1,0:T(8,128)S(1)} %copy.78, pred[192]{0:T(512)(128)(4,1)S(1)} %get-tuple-element.270, bf16[12,192,4,32]{1,3,0,2:T(8,128)(2,1)S(1)} %get-tuple-element.272, bf16[12,192,4,32]{1,3,2,0:T(8,128)(2,1)} %get-tuple-element.271, s32[]{:T(128)S(6)} %select_n.65), kind=kOutput, calls=%fused_computation.52.clone.1 | convolution fusion | flops 61046976 | bytes 3066052 | tf_op jit(solution)/shard_map/while/body/eval_jaxpr/sub | solution.py:92
  64.5 2.9 %fusion.63 = f32[12,96,4,32]{1,3,2,0:T(8,128)S(1)} fusion(bf16[12,192,4,32]{1,3,2,0:T(8,128)(2,1)} %get-tuple-element.274, bf16[4,12,96,192]{3,2,1,0:T(8,128)(2,1)} %get-tuple-element.241, f32[12,96,4]{1,2,0:T(4,128)S(1)} %copy.79), kind=kOutput, calls=%fused_computation.11.clone.1 | convolution fusion | flops 56770560 | bytes 2967552 | tf_op jit(solution)/shard_map/while/body/eval_jaxpr/hijk,ikhd->ijhd/dot_general | solution.py:95
  67.8 0.3 copy.80
  68.2 0.8 constant_dynamic-update-slice_fusion.2
  69.0 15.2 %all_to_all.36 = bf16[12,192,128]{2,0,1:T(8,128)(2,1)S(1)} all-to-all(bf16[12,192,128]{2,0,1:T(8,128)(2,1)} %get-tuple-element.281), channel_id=1, replica_groups=mesh['groups'=2,'rows'=4,'cols'=4] {'rows'}, dimensions={1} | all-to-all | bytes 1179648 | tf_op jit(solution)/shard_map/all_to_all | solution.py:106
  84.4 1.3 %convolution_add_fusion = f32[48,48,128]{2,1,0:T(8,128)} fusion(bf16[48,48,128]{2,1,0:T(8,128)(2,1)S(1)} %bitcast.71, f32[128]{0:T(128)S(1)} %copy-done.10, bf16[128,128]{1,0:T(8,128)(2,1)S(1)} %copy-done.5), kind=kOutput, calls=%fused_computation.24 | convolution fusion | flops 75792384 | bytes 1802752 | tf_op jit(solution)/shard_map/dot_general | solution.py:107
  (61 shorter events, 2.6 us)
Async XLA Ops:
  0.0 42.9 %copy-start = (bf16[128,256]{1,0:T(8,128)(2,1)S(1)}, bf16[128,256]{1,0:T(8,128)(2,1)}, u32[]{:S(2)}) copy-start(bf16[128,256]{1,0:T(8,128)(2,1)} %param.18) | copy-start | bytes 196612
  0.0 1.8 %copy-start.1 = (f32[48,48,128]{2,1,0:T(8,128)S(1)}, f32[48,48,128]{2,1,0:T(8,128)}, u32[]{:S(2)}) copy-start(f32[48,48,128]{2,1,0:T(8,128)} %param.13) | copy-start | bytes 3538948
  0.0 2.5 %copy-start.9 = (f32[128]{0:T(128)S(1)}, f32[128]{0:T(128)}, u32[]{:S(2)}) copy-start(f32[128]{0:T(128)} %param.15) | copy-start | bytes 1540
  0.0 2.5 %copy-start.8 = (f32[128]{0:T(128)S(1)}, f32[128]{0:T(128)}, u32[]{:S(2)}) copy-start(f32[128]{0:T(128)} %param.16) | copy-start | bytes 1540
  2.5 1.6 %copy-start.7 = (f32[128,4]{0,1:T(4,128)S(1)}, f32[128,4]{0,1:T(4,128)}, u32[]{:S(2)}) copy-start(f32[128,4]{0,1:T(4,128)} %param.21) | copy-start | bytes 6148
  4.0 11.5 %copy-start.14 = (u32[32]{0:T(128)S(1)}, u32[32]{0:T(128)}, u32[]{:S(2)}) copy-start(u32[32]{0:T(128)} %constant.89) | copy-start | bytes 388
  4.0 12.8 %copy-start.12 = (s32[48]{0:T(128)S(1)}, s32[48]{0:T(128)}, u32[]{:S(2)}) copy-start(s32[48]{0:T(128)} %param.14) | copy-start | bytes 580
  6.9 19.6 %collective-permute-start = (f32[4,48,48]{2,0,1:T(4,128)S(1)}, f32[4,48,48]{2,0,1:T(4,128)S(1)}, u32[]{:S(2)}, u32[]{:S(2)}) collective-permute-start(f32[4,48,48]{2,0,1:T(4,128)S(1)} %bitcast.74), channel_id=1, source_target_pairs={{0,1},{1,2},{2,3},{3,0},{4,5},{5,6},{6,7},{7,4},{8,9},{9,10},{10,1... | collective-permute-start | bytes 110600 | tf_op jit(solution)/shard_map/ppermute | solution.py:53
  10.0 16.6 %collective-permute-start.2 = (f32[4,48,48]{2,0,1:T(4,128)S(1)}, f32[4,48,48]{2,0,1:T(4,128)S(1)}, u32[]{:S(2)}, u32[]{:S(2)}) collective-permute-start(f32[4,48,48]{2,0,1:T(4,128)S(1)} %bitcast.75), channel_id=1, source_target_pairs={{1,0},{2,1},{3,2},{0,3},{5,4},{6,5},{7,6},{4,7},{9,8},{10,9},{11,1... | collective-permute-start | bytes 110600 | tf_op jit(solution)/shard_map/ppermute | solution.py:59
  12.0 30.8 %all-to-all-start = ((bf16[48,48,128]{2,1,0:T(8,128)(2,1)}), bf16[48,48,128]{2,1,0:T(8,128)(2,1)S(1)}, u32[]{:S(2)}, u32[]{:S(2)}) async-start(bf16[48,48,128]{2,1,0:T(8,128)(2,1)} %add_convert_fusion), calls=%async_computation | async-start | bytes 1179648 | tf_op jit(solution)/shard_map/all_to_all | solution.py:37
  26.5 6.5 %collective-permute-start.1 = (f32[4,48,48]{2,0,1:T(4,128)S(1)}, f32[4,48,48]{2,0,1:T(4,128)S(1)}, u32[]{:S(2)}, u32[]{:S(2)}) collective-permute-start(f32[4,48,48]{2,0,1:T(4,128)S(1)} %collective-permute-done), channel_id=1, source_target_pairs={{0,1},{1,2},{2,3},{3,0},{4,5},{5,6},{6,7},{7,4},{8,9},{9,10},{10,1... | collective-permute-start | bytes 110600 | tf_op jit(solution)/shard_map/ppermute | solution.py:53
  43.9 2.2 %copy-start.6 = (bf16[128,128]{1,0:T(8,128)(2,1)S(1)}, bf16[128,128]{1,0:T(8,128)(2,1)}, u32[]{:S(2)}) copy-start(bf16[128,128]{1,0:T(8,128)(2,1)} %param.17) | copy-start | bytes 98308
  46.1 1.5 %copy-start.11 = (bf16[128,128]{1,0:T(8,128)(2,1)S(1)}, bf16[128,128]{1,0:T(8,128)(2,1)}, u32[]{:S(2)}) copy-start(bf16[128,128]{1,0:T(8,128)(2,1)} %param.19) | copy-start | bytes 98308
  46.1 1.5 %copy-start.13 = (f32[128]{0:T(128)S(1)}, f32[128]{0:T(128)}, u32[]{:S(2)}) copy-start(f32[128]{0:T(128)} %param.20) | copy-start | bytes 1540
  47.6 2.5 %copy-start.3 = (bf16[12,192,4,32]{1,3,0,2:T(8,128)(2,1)S(1)}, bf16[12,192,4,32]{1,3,0,2:T(8,128)(2,1)}, u32[]{:S(2)}) copy-start(bf16[12,192,4,32]{1,3,0,2:T(8,128)(2,1)} %copy.40) | copy-start | bytes 1769476
  55.0 2.9 %copy-start.2 = (f32[12,192,128]{2,1,0:T(8,128)S(1)}, f32[12,192,128]{2,1,0:T(8,128)}, u32[]{:S(2)}) copy-start(f32[12,192,128]{2,1,0:T(8,128)} %get-tuple-element.269) | copy-start | bytes 3538948 | tf_op jit(solution)/shard_map/while
  58.4 1.2 %copy-start.4 = (bf16[12,192,4,32]{1,3,0,2:T(8,128)(2,1)S(1)}, bf16[12,192,4,32]{1,3,0,2:T(8,128)(2,1)}, u32[]{:S(2)}) copy-start(bf16[12,192,4,32]{1,3,0,2:T(8,128)(2,1)} %get-tuple-element.292) | copy-start | bytes 1769476 | tf_op jit(solution)/shard_map/while
  64.5 2.9 %copy-start.2 = (f32[12,192,128]{2,1,0:T(8,128)S(1)}, f32[12,192,128]{2,1,0:T(8,128)}, u32[]{:S(2)}) copy-start(f32[12,192,128]{2,1,0:T(8,128)} %get-tuple-element.269) | copy-start | bytes 3538948 | tf_op jit(solution)/shard_map/while
  67.8 1.2 %copy-start.4 = (bf16[12,192,4,32]{1,3,0,2:T(8,128)(2,1)S(1)}, bf16[12,192,4,32]{1,3,0,2:T(8,128)(2,1)}, u32[]{:S(2)}) copy-start(bf16[12,192,4,32]{1,3,0,2:T(8,128)(2,1)} %get-tuple-element.292) | copy-start | bytes 1769476 | tf_op jit(solution)/shard_map/while
  69.0 15.4 %copy-start.5 = (bf16[128,128]{1,0:T(8,128)(2,1)S(1)}, bf16[128,128]{1,0:T(8,128)(2,1)}, u32[]{:S(2)}) copy-start(bf16[128,128]{1,0:T(8,128)(2,1)} %param.22) | copy-start | bytes 98308
  69.0 15.4 %copy-start.10 = (f32[128]{0:T(128)S(1)}, f32[128]{0:T(128)}, u32[]{:S(2)}) copy-start(f32[128]{0:T(128)} %param.23) | copy-start | bytes 1540
